TPU v7x, 128 devices: a whole 4x4x4 slice. The times are simulated.
128 devices in a mesh: ctx: 32 (over z, y_lo, x), grp: 4 (over y_hi, core).
Axes of the slice: x: 4, y: 4 (y_hi: 2, y_lo: 2; y = y_hi * 2 + y_lo), z: 4, core: 2. Of those that a mesh axis runs over, the one named last changes fastest.
Arguments:
- query_input: bfloat16 [16384, 4096], P(('ctx', 'grp')), may hold values from -6 to 6
- key_input: bfloat16 [16384, 4096], P(('ctx', 'grp')), may hold values from -6 to 6
- value_input: bfloat16 [16384, 4096], P(('ctx', 'grp')), may hold values from -6 to 6
- out_grad: bfloat16 [16384, 4096], P(('ctx', 'grp')), may hold values from -6 to 6
- residues: float32 [8, 16], replicated, may hold values from -2 to 2
- decay_rates: float32 [8, 16], replicated, may hold values from 3.0517578e-06 to 0.15
Outputs:
- output: float32 [16384, 4096], P(('ctx', 'grp'))
- query_grad: float32 [16384, 4096], P(('ctx', 'grp'))
- key_grad: float32 [16384, 4096], P(('ctx', 'grp'))
- value_grad: float32 [16384, 4096], P(('ctx', 'grp'))
- residue_grad: float32 [8, 16], replicated
All inputs are finite; a program needn't handle non-finite values.
Results may differ from a plain program's by a relative error of at most 0.0055.
Values may be sent and summed in bfloat16 or wider, within the bound.
A program may use at most 192 MiB of HBM per device.

v0:
```python
import math
import jax
import jax.numpy as jnp
from jax import lax
from jax.sharding import PartitionSpec as P

GROUP = 512
HIGHEST = lax.Precision.HIGHEST


def entering(part, axis, combine, identity, reverse):
    count = lax.axis_size(axis)
    place = lax.axis_index(axis)
    ahead = count - 1 - place if reverse else place
    gathered = jax.tree.map(lambda a: lax.all_gather(a, axis), part)
    state = jax.tree.map(lambda a, e: jnp.zeros_like(a) + jnp.asarray(e, a.dtype), part, identity)

    def one(hop, state):
        source = count - 1 - hop if reverse else hop
        return combine(
            state, jax.tree.map(lambda a: lax.dynamic_index_in_dim(a, source, 0, False), gathered)
        )

    return lax.fori_loop(0, ahead, one, state)


def mode_tables(term_residues, decays, pairing, span):
    position = jnp.arange(span).astype(jnp.float32)
    distance = position[:, None] - position[None, :]
    causal_mask = distance >= 0.0
    lag_values = jnp.maximum(distance, 0.0)
    group_count = term_residues.shape[0]

    def one_mode(total, columns):
        res_column, decay_column = columns
        weight = jnp.where(
            causal_mask[None], jnp.exp(-decay_column[:, None, None] * lag_values[None]), 0.0
        )
        total = total + res_column[:, None, None] * weight
        return (total, jnp.sum(pairing * weight, axis=(1, 2)))

    start_total = jnp.zeros((group_count, span, span), jnp.float32)
    causal, inside = lax.scan(one_mode, start_total, (term_residues.T, decays.T))
    upper_part = causal.astype(jnp.bfloat16)
    lower_part = (causal - upper_part.astype(jnp.float32)).astype(jnp.bfloat16)
    return (upper_part, lower_part, inside.T)


def link_states(earlier, later):
    return (later[1][:, :, None] * earlier[0] + later[0], earlier[1] * later[1])


def convolve(product, inner_grad, term_residues, decays, carry_states):
    span, columns = product.shape
    group_count = columns // GROUP
    grouped = product.reshape(span, group_count, GROUP)
    grad_rows = inner_grad.reshape(span, group_count, GROUP)
    pairing = jnp.einsum("agc,bgc->gab", grad_rows, grouped, preferred_element_type=jnp.float32)
    upper_part, lower_part, inside = mode_tables(term_residues, decays, pairing, span)
    mixed_sum = jnp.einsum("gab,bgc->agc", upper_part, grouped, preferred_element_type=jnp.float32)
    mixed_sum = mixed_sum + jnp.einsum(
        "gab,bgc->agc", lower_part, grouped, preferred_element_type=jnp.float32
    )
    conv_sum = jnp.einsum("gab,agc->bgc", upper_part, grad_rows, preferred_element_type=jnp.float32)
    conv_sum = conv_sum + jnp.einsum(
        "gab,agc->bgc", lower_part, grad_rows, preferred_element_type=jnp.float32
    )
    position = jnp.arange(span).astype(jnp.float32)
    to_end = jnp.exp(-decays[:, :, None] * (span - 1.0 - position)[None, None, :])
    from_start = jnp.exp(-decays[:, :, None] * position[None, None, :])
    end_states = jnp.einsum("gmb,bgc->gmc", to_end, grouped.astype(jnp.float32), precision=HIGHEST)
    start_states = jnp.einsum(
        "gma,agc->gmc", from_start, grad_rows.astype(jnp.float32), precision=HIGHEST
    )
    factor = jnp.exp(-decays * float(span))
    carried_in, behind = carry_states(end_states, start_states, factor, span)
    rising = jnp.exp(-decays[:, :, None] * (position + 1.0)[None, None, :])
    falling = jnp.exp(-decays[:, :, None] * (span - position)[None, None, :])
    mixed_sum = mixed_sum + jnp.einsum(
        "gma,gmc->agc", term_residues[:, :, None] * rising, carried_in, precision=HIGHEST
    )
    conv_sum = conv_sum + jnp.einsum(
        "gmb,gmc->bgc", term_residues[:, :, None] * falling, behind, precision=HIGHEST
    )
    projected = jnp.einsum(
        "agc,gmc->gma", grad_rows.astype(jnp.float32), carried_in, precision=HIGHEST
    )
    residue_share = inside + jnp.sum(projected * rising, axis=2)
    return (mixed_sum.reshape(span, columns), conv_sum.reshape(span, columns), residue_share)


def finish(query_part, key_part, value_part, grad_part, mixed_out, conv_grad):
    output = query_part.astype(jnp.float32) * mixed_out
    query_grad = grad_part.astype(jnp.float32) * mixed_out
    key_grad = conv_grad * value_part.astype(jnp.float32)
    value_grad = conv_grad * key_part.astype(jnp.float32)
    return (output, query_grad, key_grad, value_grad)


def gated_inputs(query_input, key_input, value_input, out_grad):
    product = (key_input.astype(jnp.float32) * value_input.astype(jnp.float32)).astype(jnp.bfloat16)
    inner_grad = (out_grad.astype(jnp.float32) * query_input.astype(jnp.float32)).astype(
        jnp.bfloat16
    )
    return (product, inner_grad)


def channel_layout(query_input, key_input, value_input, out_grad, residues, decay_rates):
    product, inner_grad = gated_inputs(query_input, key_input, value_input, out_grad)
    prod_cols, grad_cols = (
        lax.all_to_all(product, "grp", split_axis=1, concat_axis=0, tiled=True),
        lax.all_to_all(inner_grad, "grp", split_axis=1, concat_axis=0, tiled=True),
    )
    row_count, columns = prod_cols.shape
    group_count = columns // GROUP
    first_group = lax.axis_index("grp") * group_count
    local_res = lax.dynamic_slice_in_dim(residues, first_group, group_count, 0)
    local_decay = lax.dynamic_slice_in_dim(decay_rates, first_group, group_count, 0)

    def carry_states(end_states, start_states, factor, span):
        neutral = (jnp.zeros_like(end_states), jnp.ones_like(factor))
        carried_in, spent_ahead = entering((end_states, factor), "ctx", link_states, neutral, False)
        behind, spent_behind = entering((start_states, factor), "ctx", link_states, neutral, True)
        return (carried_in, behind)

    mixed_cols, conv_cols, residue_share = convolve(
        prod_cols, grad_cols, local_res, local_decay, carry_states
    )
    mixed_rows, conv_rows = (
        lax.all_to_all(mixed_cols, "grp", split_axis=0, concat_axis=1, tiled=True),
        lax.all_to_all(conv_cols, "grp", split_axis=0, concat_axis=1, tiled=True),
    )
    results = finish(query_input, key_input, value_input, out_grad, mixed_rows, conv_rows)
    placed = lax.dynamic_update_slice_in_dim(
        jnp.zeros(residues.shape, jnp.float32), residue_share, first_group, 0
    )
    return (results, placed, row_count * lax.axis_size("ctx"))


def on_device(query_input, key_input, value_input, out_grad, residues, decay_rates):
    results, placed, length = channel_layout(
        query_input, key_input, value_input, out_grad, residues, decay_rates
    )
    summed = lax.psum(placed, ("ctx", "grp"))
    residue_grad = summed / (length * math.sqrt(GROUP))
    return (results[0], results[1], results[2], results[3], residue_grad)


def solution(mesh):
    in_specs = (
        P(("ctx", "grp"), None),
        P(("ctx", "grp"), None),
        P(("ctx", "grp"), None),
        P(("ctx", "grp"), None),
        P(),
        P(),
    )
    out_specs = (
        P(("ctx", "grp"), None),
        P(("ctx", "grp"), None),
        P(("ctx", "grp"), None),
        P(("ctx", "grp"), None),
        P(),
    )
    return jax.shard_map(
        on_device, mesh=mesh, in_specs=in_specs, out_specs=out_specs, check_vma=False
    )
```

profile of v0, /device:TPU:1, one launch (start us, length us, event | category | flops | bytes accessed | tf_op | source)
XLA Modules:
  0.0 491.0 jit_solution(2044057091201564266)
XLA Ops:
  10.0 6.0 %all-to-all-start.1 = ((bf16[128,4,1024]{2,0,1:T(8,128)(2,1)}), bf16[128,4,1024]{2,0,1:T(8,128)(2,1)S(1)}, u32[]{:S(2)}, u32[]{:S(2)}) async-start(bf16[128,4,1024]{2,0,1:T(8,128)(2,1)} %bitcast.53), calls=%async_computation.1 | async-start | bytes 2097152 | tf_op jit(solution)/shard_map/all_to_all | solution.py:112
  16.9 14.2 %all-to-all-done.1 = bf16[128,4,1024]{2,0,1:T(8,128)(2,1)S(1)} async-done(((bf16[128,4,1024]{2,0,1:T(8,128)(2,1)}), bf16[128,4,1024]{2,0,1:T(8,128)(2,1)S(1)}, u32[]{:S(2)}, u32[]{:S(2)}) %all-to-all-start.1) | async-done | bytes 1048608 | tf_op jit(solution)/shard_map/all_to_all | solution.py:112
  36.5 5.1 %all-to-all-start = ((bf16[128,4,1024]{2,0,1:T(8,128)(2,1)}), bf16[128,4,1024]{2,0,1:T(8,128)(2,1)}, u32[]{:S(2)}, u32[]{:S(2)}) async-start(bf16[128,4,1024]{2,0,1:T(8,128)(2,1)} %bitcast.54), calls=%async_computation | async-start | bytes 2097152 | tf_op jit(solution)/shard_map/all_to_all | solution.py:111
  41.7 68.3 %all-gather.3 = f32[32,2,16]{2,1,0:T(2,128)S(1)} all-gather(f32[1,2,16]{2,1,0:T(2,128)S(1)} %get-tuple-element.293), channel_id=2, replica_groups=mesh['ctx'=32,'grp'=4] {'ctx'}, dimensions={0}, use_global_device_ids=true | all-gather | bytes 4224 | tf_op jit(solution)/shard_map/all_gather | solution.py:15
  115.1 3.3 fusion.9
  118.4 54.7 %while.43 = (s32[]{:T(128)}, f32[2,512,512]{2,1,0:T(8,128)S(1)}, f32[16,2]{1,0:T(8,128)S(1)}, f32[16,2]{1,0:T(8,128)S(1)}, f32[16,2]{1,0:T(8,128)S(1)}, /*index=...) while((s32[]{:T(128)}, f32[2,512,512]{2,1,0:T(8,128)S(1)}, ...), condition=%wide.region_2.3_spmd.clone.clone.clone, body=%wide.region_0.2_spmd.clone.clone.clone.sunk | while | flops 4718595 | bytes 8917183 | solution.py:43
  118.9 3.0 multiply_reduce_fusion.2
  122.3 3.0 multiply_reduce_fusion.2
  125.7 3.0 multiply_reduce_fusion.2
  129.1 3.0 multiply_reduce_fusion.2
  132.5 3.0 multiply_reduce_fusion.2
  135.9 3.0 multiply_reduce_fusion.2
  139.4 3.0 multiply_reduce_fusion.2
  142.8 3.0 multiply_reduce_fusion.2
  146.2 3.0 multiply_reduce_fusion.2
  149.6 3.0 multiply_reduce_fusion.2
  159.9 3.0 multiply_reduce_fusion.2
  163.3 3.0 multiply_reduce_fusion.2
  166.7 3.0 multiply_reduce_fusion.2
  170.1 3.0 multiply_reduce_fusion.2
  175.6 3.7 copy.71
  179.2 3.4 fusion.39
  188.8 28.8 %while.42 = (s32[]{:T(128)}, f32[2,16,512]{2,1,0:T(8,128)S(1)}, s32[]{:T(128)}, f32[32,2,16]{2,1,0:T(2,128)S(1)}, f32[32,2,16,512]{3,2,1,0:T(8,128)}, /*index=5*/s32[]{:T(128)}, s32[]{:T(128)}, s32[]{:T(128)}, s32[]{:T(128)}) while((s32[]{:T(128)}, f32[2,16,512]{2,1,0:T(8,128)S(1)}, s32[]{:T(128)}, f32[32,2,16]{2,1,0:T(2,128)S(1)}, ...), condition=%wide.region_6.7_spmd, body=%wide.region_5.6_spmd.sunk | while | flops 32774 | bytes 197147 | solution.py:24
  217.6 5.5 %add_bitcast_fusion = f32[512,2,512]{0,2,1:T(8,128)} fusion(f32[2,512,512]{2,1,0:T(8,128)} %fusion.39, f32[2,512,512]{2,1,0:T(8,128)} %fusion.43, f32[2,16,512]{2,1,0:T(8,128)S(1)} %get-tuple-element.178, f32[512]{0:T(512)S(1)} %fusion.35, f32[2,16]{1,0:T(2,128)S(1)} %constant_dynamic-slice_fusion.1, f32[2,16]{1,0:T(2,128)S(1)} %get-tuple-element.294), kind=kOutput, calls=%fused_computation.21 | convolution fusion | flops 101744640 | bytes 6359296 | tf_op jit(solution)/shard_map/gmb,gmc->bgc/dot_general | solution.py:82
  226.5 18.8 %all-to-all-start.3 = ((f32[4,128,1024]{1,2,0:T(8,128)}), f32[4,128,1024]{1,2,0:T(8,128)S(1)}, u32[]{:S(2)}, u32[]{:S(2)}) async-start(f32[4,128,1024]{1,2,0:T(8,128)} %copy.81), calls=%async_computation.3 | async-start | bytes 4194304 | tf_op jit(solution)/shard_map/all_to_all | solution.py:131
  245.3 77.5 %all-gather.7.cloned.1.call-done = f32[64,16,512]{2,1,0:T(8,128)} async-done(((f32[2,16,512]{2,1,0:T(8,128)}), f32[64,16,512]{2,1,0:T(8,128)}) %all-gather.7.cloned.1.call-update) | async-done | bytes 2097168 | tf_op jit(solution)/shard_map/all_gather | solution.py:15
  322.9 5.5 %add_bitcast_fusion.1 = f32[512,2,512]{0,2,1:T(8,128)} fusion(f32[2,512,512]{2,1,0:T(8,128)} %fusion.41, f32[2,512,512]{2,1,0:T(8,128)} %fusion.44, f32[2,16,512]{2,1,0:T(8,128)S(1)} %get-tuple-element.177, f32[512]{0:T(512)S(1)} %fusion.33, f32[2,16]{1,0:T(2,128)S(1)} %constant_dynamic-slice_fusion.1, f32[2,16]{1,0:T(2,128)S(1)} %get-tuple-element.294), kind=kOutput, calls=%fused_computation.22 | convolution fusion | flops 101744640 | bytes 6359296 | tf_op jit(solution)/shard_map/gma,gmc->agc/dot_general | solution.py:79
  331.2 3.0 copy.75
  334.3 26.2 %all-to-all-start.2 = ((f32[4,128,1024]{1,2,0:T(8,128)}), f32[4,128,1024]{1,2,0:T(8,128)}, u32[]{:S(2)}, u32[]{:S(2)}) async-start(f32[4,128,1024]{1,2,0:T(8,128)} %copy.75), calls=%async_computation.2 | async-start | bytes 4194304 | tf_op jit(solution)/shard_map/all_to_all | solution.py:130
  361.6 110.7 %psum.7 = f32[8,16]{1,0:T(8,128)S(1)} all-reduce(f32[8,16]{1,0:T(8,128)S(1)} %fusion.36), channel_id=1, replica_groups=mesh['ctx'=32,'grp'=4] {'ctx','grp'}, use_global_device_ids=true, to_apply=%region_8.9 | all-reduce | flops 128 | bytes 1024 | tf_op jit(solution)/shard_map/psum | solution.py:144
  474.8 3.0 copy.76
  477.8 6.3 %convert_multiply_fusion = (f32[128,4096]{1,0:T(8,128)}, f32[128,4096]{1,0:T(8,128)}, f32[128,4096]{1,0:T(8,128)}, f32[128,4096]{1,0:T(8,128)}) fusion(f32[128,4096]{1,0:T(8,128)} %copy.76, bf16[128,4096]{1,0:T(8,128)(2,1)} %param.15, bf16[128,4096]{1,0:T(8,128)(2,1)} %param.12, f32[128,4096]{1,0:T(8,128)S(1)} %copy-done.3, ...), kind=kLoop, calls=%fused_computation.13 | loop fusion | flops 4194304 | bytes 16777216 | tf_op jit(solution)/shard_map/mul | solution.py:94
  (186 shorter events, 74.1 us)
Async XLA Ops:
  7.2 34.5 %copy-start = (f32[8,16]{1,0:T(8,128)S(1)}, f32[8,16]{1,0:T(8,128)}, u32[]{:S(2)}) copy-start(f32[8,16]{1,0:T(8,128)} %param.16) | copy-start | bytes 1540
  10.0 21.1 %all-to-all-start.1 = ((bf16[128,4,1024]{2,0,1:T(8,128)(2,1)}), bf16[128,4,1024]{2,0,1:T(8,128)(2,1)S(1)}, u32[]{:S(2)}, u32[]{:S(2)}) async-start(bf16[128,4,1024]{2,0,1:T(8,128)(2,1)} %bitcast.53), calls=%async_computation.1 | async-start | bytes 2097152 | tf_op jit(solution)/shard_map/all_to_all | solution.py:112
  16.0 19.1 %copy-start.4 = (bf16[128,4096]{1,0:T(8,128)(2,1)S(1)}, bf16[128,4096]{1,0:T(8,128)(2,1)}, u32[]{:S(2)}) copy-start(bf16[128,4096]{1,0:T(8,128)(2,1)} %param.14) | copy-start | bytes 3145732
  16.0 19.2 %copy-start.6 = (bf16[128,4096]{1,0:T(8,128)(2,1)S(1)}, bf16[128,4096]{1,0:T(8,128)(2,1)}, u32[]{:S(2)}) copy-start(bf16[128,4096]{1,0:T(8,128)(2,1)} %param.13) | copy-start | bytes 3145732
  16.0 172.8 %all-gather.9.cloned.1.call-start = ((), (), s32[]{:S(2)}) async-start(), calls=%async_computation.5 | async-start | bytes 2162688 | tf_op jit(solution)/shard_map/all_gather | solution.py:15
  31.1 1.0 copy-start.7
  36.5 73.6 %all-to-all-start = ((bf16[128,4,1024]{2,0,1:T(8,128)(2,1)}), bf16[128,4,1024]{2,0,1:T(8,128)(2,1)}, u32[]{:S(2)}, u32[]{:S(2)}) async-start(bf16[128,4,1024]{2,0,1:T(8,128)(2,1)} %bitcast.54), calls=%async_computation | async-start | bytes 2097152 | tf_op jit(solution)/shard_map/all_to_all | solution.py:111
  41.6 281.3 %all-gather.7.cloned.1.call-start = ((), (), s32[]{:S(2)}) async-start(), calls=%async_computation.4 | async-start | bytes 2162688 | tf_op jit(solution)/shard_map/all_gather | solution.py:15
  179.2 3.4 copy-start.2
  182.6 2.1 copy-start.1
  226.5 107.8 %all-to-all-start.3 = ((f32[4,128,1024]{1,2,0:T(8,128)}), f32[4,128,1024]{1,2,0:T(8,128)S(1)}, u32[]{:S(2)}, u32[]{:S(2)}) async-start(f32[4,128,1024]{1,2,0:T(8,128)} %copy.81), calls=%async_computation.3 | async-start | bytes 4194304 | tf_op jit(solution)/shard_map/all_to_all | solution.py:131
  334.3 140.5 %all-to-all-start.2 = ((f32[4,128,1024]{1,2,0:T(8,128)}), f32[4,128,1024]{1,2,0:T(8,128)}, u32[]{:S(2)}, u32[]{:S(2)}) async-start(f32[4,128,1024]{1,2,0:T(8,128)} %copy.75), calls=%async_computation.2 | async-start | bytes 4194304 | tf_op jit(solution)/shard_map/all_to_all | solution.py:130
  474.8 3.0 copy-start.3
  474.8 3.0 copy-start.5
Sparse Core Ops, SparseCore 0:
  35.3 132.3 all-gather.8
  169.3 153.5 all-gather.6
where the time goes:
time: 494 us; the launch traced here: 491 us
  blocking collectives  179 us (36%)
  other arithmetic  91.8 us (19%)
  waiting for transfers between devices  91.8 us (19%)
  starting transfers between devices  56.1 us (11%)
  local copies, waits for them, and re-layouts  28.8 us (6%)
  matrix products  28.5 us (6%)
  between operations  14.1 us (3%)
    psum x1, blocking collectives, on_device(): summed = lax.psum(placed, ('ctx', 'grp'))  111 us
    all_gather x2, waiting for transfers between devices, entering(): gathered = jax.tree.map(lambda a: lax.all_gather(a, axis), part)  77.6 us
    all_gather x1, blocking collectives, entering(): gathered = jax.tree.map(lambda a: lax.all_gather(a, axis), part)  68.3 us
    reduce_sum x16, other arithmetic, one_mode(): return (total, jnp.sum(pairing * weight, axis=(1, 2)))  47.3 us
    add x31, other arithmetic, link_states(): return (later[1][:, :, None] * earlier[0] + later[0], earlier[1] * later[1])  28.6 us
    all_to_all x1, starting transfers between devices, channel_layout(): lax.all_to_all(mixed_cols, 'grp', split_axis=0, concat_axis=1, tiled=True)  26.2 us
    all_to_all x1, starting transfers between devices, channel_layout(): lax.all_to_all(conv_cols, 'grp', split_axis=0, concat_axis=1, tiled=True)  18.8 us
    all_to_all x1, waiting for transfers between devices, channel_layout(): lax.all_to_all(inner_grad, 'grp', split_axis=1, concat_axis=0, tiled=True)  14.2 us
  transfers between devices with their start and end apart: 6, of which 2 were waited for; matrix products, arithmetic and copies ran while one was open for 26% of the time, Pallas kernels for 0%

commit v1 on v0

--- a/solution.py
+++ b/solution.py
@@ -141,7 +141,7 @@
     results, placed, length = channel_layout(
         query_input, key_input, value_input, out_grad, residues, decay_rates
     )
-    summed = lax.psum(placed, ("ctx", "grp"))
+    summed = lax.psum(lax.psum(placed, "grp"), "ctx")
     residue_grad = summed / (length * math.sqrt(GROUP))
     return (results[0], results[1], results[2], results[3], residue_grad)
 

time: 494 us -> 521 us (1.055)
  the two profiles are of different devices: /device:TPU:1 before, /device:TPU:16 now
where the time goes in v1:
time: 521 us; the launch traced here: 518 us
  blocking collectives  221 us (42%)
  waiting for transfers between devices  111 us (21%)
  other arithmetic  91.9 us (18%)
  local copies, waits for them, and re-layouts  28.8 us (6%)
  matrix products  28.4 us (5%)
  starting transfers between devices  22.3 us (4%)
  between operations  14.1 us (3%)
    psum x2, blocking collectives, on_device(): summed = lax.psum(lax.psum(placed, 'grp'), 'ctx')  139 us
    all_gather x2, waiting for transfers between devices, entering(): gathered = jax.tree.map(lambda a: lax.all_gather(a, axis), part)  98.5 us
    all_gather x1, blocking collectives, entering(): gathered = jax.tree.map(lambda a: lax.all_gather(a, axis), part)  82.3 us
    reduce_sum x16, other arithmetic, one_mode(): return (total, jnp.sum(pairing * weight, axis=(1, 2)))  47.3 us
    add x31, other arithmetic, link_states(): return (later[1][:, :, None] * earlier[0] + later[0], earlier[1] * later[1])  28.6 us
    all_to_all x1, waiting for transfers between devices, channel_layout(): lax.all_to_all(inner_grad, 'grp', split_axis=1, concat_axis=0, tiled=True)  11.9 us
  transfers between devices with their start and end apart: 6, of which 2 were waited for; matrix products, arithmetic and copies ran while one was open for 25% of the time, Pallas kernels for 0%

profile of v1, /device:TPU:16, one launch (start us, length us, event | category | flops | bytes accessed | tf_op | source)
XLA Modules:
  0.0 518.0 jit_solution(4828907622907540834)
XLA Ops:
  10.0 4.8 all-to-all-start.1
  15.7 11.9 %all-to-all-done.1 = bf16[128,4,1024]{2,0,1:T(8,128)(2,1)S(1)} async-done(((bf16[128,4,1024]{2,0,1:T(8,128)(2,1)}), bf16[128,4,1024]{2,0,1:T(8,128)(2,1)S(1)}, u32[]{:S(2)}, u32[]{:S(2)}) %all-to-all-start.1) | async-done | bytes 1048608 | tf_op jit(solution)/shard_map/all_to_all | solution.py:112
  33.0 7.4 %all-to-all-start = ((bf16[128,4,1024]{2,0,1:T(8,128)(2,1)}), bf16[128,4,1024]{2,0,1:T(8,128)(2,1)}, u32[]{:S(2)}, u32[]{:S(2)}) async-start(bf16[128,4,1024]{2,0,1:T(8,128)(2,1)} %bitcast.54), calls=%async_computation | async-start | bytes 2097152 | tf_op jit(solution)/shard_map/all_to_all | solution.py:111
  40.6 82.3 %all-gather.3 = f32[32,2,16]{2,1,0:T(2,128)S(1)} all-gather(f32[1,2,16]{2,1,0:T(2,128)S(1)} %get-tuple-element.293), channel_id=2, replica_groups=mesh['ctx'=32,'grp'=4] {'ctx'}, dimensions={0}, use_global_device_ids=true | all-gather | bytes 4224 | tf_op jit(solution)/shard_map/all_gather | solution.py:15
  127.9 3.3 fusion.9
  131.2 54.7 %while.43 = (s32[]{:T(128)}, f32[2,512,512]{2,1,0:T(8,128)S(1)}, f32[16,2]{1,0:T(8,128)S(1)}, f32[16,2]{1,0:T(8,128)S(1)}, f32[16,2]{1,0:T(8,128)S(1)}, /*index=...) while((s32[]{:T(128)}, f32[2,512,512]{2,1,0:T(8,128)S(1)}, ...), condition=%wide.region_2.3_spmd.clone.clone.clone, body=%wide.region_0.2_spmd.clone.clone.clone.sunk | while | flops 4718595 | bytes 8917183 | solution.py:43
  131.6 3.0 multiply_reduce_fusion.2
  135.0 3.0 multiply_reduce_fusion.2
  138.5 3.0 multiply_reduce_fusion.2
  141.9 3.0 multiply_reduce_fusion.2
  145.3 3.0 multiply_reduce_fusion.2
  148.7 3.0 multiply_reduce_fusion.2
  152.1 3.0 multiply_reduce_fusion.2
  155.6 3.0 multiply_reduce_fusion.2
  162.4 3.0 multiply_reduce_fusion.2
  165.8 3.0 multiply_reduce_fusion.2
  172.7 3.0 multiply_reduce_fusion.2
  176.1 3.0 multiply_reduce_fusion.2
  182.9 3.0 multiply_reduce_fusion.2
  188.4 3.7 copy.71
  192.1 3.4 fusion.39
  201.7 28.8 %while.42 = (s32[]{:T(128)}, f32[2,16,512]{2,1,0:T(8,128)S(1)}, s32[]{:T(128)}, f32[32,2,16]{2,1,0:T(2,128)S(1)}, f32[32,2,16,512]{3,2,1,0:T(8,128)}, /*index=5*/s32[]{:T(128)}, s32[]{:T(128)}, s32[]{:T(128)}, s32[]{:T(128)}) while((s32[]{:T(128)}, f32[2,16,512]{2,1,0:T(8,128)S(1)}, s32[]{:T(128)}, f32[32,2,16]{2,1,0:T(2,128)S(1)}, ...), condition=%wide.region_6.7_spmd, body=%wide.region_5.6_spmd.sunk | while | flops 32774 | bytes 197147 | solution.py:24
  230.4 5.5 %add_bitcast_fusion = f32[512,2,512]{0,2,1:T(8,128)} fusion(f32[2,512,512]{2,1,0:T(8,128)} %fusion.39, f32[2,512,512]{2,1,0:T(8,128)} %fusion.43, f32[2,16,512]{2,1,0:T(8,128)S(1)} %get-tuple-element.178, f32[512]{0:T(512)S(1)} %fusion.35, f32[2,16]{1,0:T(2,128)S(1)} %constant_dynamic-slice_fusion.1, f32[2,16]{1,0:T(2,128)S(1)} %get-tuple-element.294), kind=kOutput, calls=%fused_computation.21 | convolution fusion | flops 101744640 | bytes 6359296 | tf_op jit(solution)/shard_map/gmb,gmc->bgc/dot_general | solution.py:82
  239.3 4.8 all-to-all-start.3
  244.1 98.5 %all-gather.7.cloned.1.call-done = f32[64,16,512]{2,1,0:T(8,128)} async-done(((f32[2,16,512]{2,1,0:T(8,128)}), f32[64,16,512]{2,1,0:T(8,128)}) %all-gather.7.cloned.1.call-update) | async-done | bytes 2097168 | tf_op jit(solution)/shard_map/all_gather | solution.py:15
  342.7 5.5 %add_bitcast_fusion.1 = f32[512,2,512]{0,2,1:T(8,128)} fusion(f32[2,512,512]{2,1,0:T(8,128)} %fusion.41, f32[2,512,512]{2,1,0:T(8,128)} %fusion.44, f32[2,16,512]{2,1,0:T(8,128)S(1)} %get-tuple-element.177, f32[512]{0:T(512)S(1)} %fusion.33, f32[2,16]{1,0:T(2,128)S(1)} %constant_dynamic-slice_fusion.1, f32[2,16]{1,0:T(2,128)S(1)} %get-tuple-element.294), kind=kOutput, calls=%fused_computation.22 | convolution fusion | flops 101744640 | bytes 6359296 | tf_op jit(solution)/shard_map/gma,gmc->agc/dot_general | solution.py:79
  351.0 3.0 copy.75
  354.1 5.3 %all-to-all-start.2 = ((f32[4,128,1024]{1,2,0:T(8,128)}), f32[4,128,1024]{1,2,0:T(8,128)}, u32[]{:S(2)}, u32[]{:S(2)}) async-start(f32[4,128,1024]{1,2,0:T(8,128)} %copy.75), calls=%async_computation.2 | async-start | bytes 4194304 | tf_op jit(solution)/shard_map/all_to_all | solution.py:130
  360.5 27.3 %psum.14 = f32[8,16]{1,0:T(8,128)S(1)} all-reduce(f32[8,16]{1,0:T(8,128)S(1)} %fusion.36), channel_id=1, replica_groups=mesh['ctx'=32,'grp'=4] {'grp'}, use_global_device_ids=true, to_apply=%region_8.9 | all-reduce | flops 128 | bytes 1024 | tf_op jit(solution)/shard_map/psum | solution.py:144
  387.8 111.6 %psum.15 = f32[8,16]{1,0:T(8,128)S(1)} all-reduce(f32[8,16]{1,0:T(8,128)S(1)} %psum.14), channel_id=1, replica_groups=mesh['ctx'=32,'grp'=4] {'ctx'}, use_global_device_ids=true, to_apply=%region_9.10 | all-reduce | flops 128 | bytes 1024 | tf_op jit(solution)/shard_map/psum | solution.py:144
  501.8 3.0 copy.76
  504.8 6.3 %convert_multiply_fusion = (f32[128,4096]{1,0:T(8,128)}, f32[128,4096]{1,0:T(8,128)}, f32[128,4096]{1,0:T(8,128)}, f32[128,4096]{1,0:T(8,128)}) fusion(f32[128,4096]{1,0:T(8,128)} %copy.76, bf16[128,4096]{1,0:T(8,128)(2,1)} %param.15, bf16[128,4096]{1,0:T(8,128)(2,1)} %param.12, f32[128,4096]{1,0:T(8,128)S(1)} %copy-done.3, ...), kind=kLoop, calls=%fused_computation.13 | loop fusion | flops 4194304 | bytes 16777216 | tf_op jit(solution)/shard_map/mul | solution.py:94
  (187 shorter events, 77.0 us)
Async XLA Ops:
  7.2 33.3 %copy-start = (f32[8,16]{1,0:T(8,128)S(1)}, f32[8,16]{1,0:T(8,128)}, u32[]{:S(2)}) copy-start(f32[8,16]{1,0:T(8,128)} %param.16) | copy-start | bytes 1540
  10.0 17.6 %all-to-all-start.1 = ((bf16[128,4,1024]{2,0,1:T(8,128)(2,1)}), bf16[128,4,1024]{2,0,1:T(8,128)(2,1)S(1)}, u32[]{:S(2)}, u32[]{:S(2)}) async-start(bf16[128,4,1024]{2,0,1:T(8,128)(2,1)} %bitcast.53), calls=%async_computation.1 | async-start | bytes 2097152 | tf_op jit(solution)/shard_map/all_to_all | solution.py:112
  14.8 16.8 %copy-start.4 = (bf16[128,4096]{1,0:T(8,128)(2,1)S(1)}, bf16[128,4096]{1,0:T(8,128)(2,1)}, u32[]{:S(2)}) copy-start(bf16[128,4096]{1,0:T(8,128)(2,1)} %param.14) | copy-start | bytes 3145732
  14.8 16.8 %copy-start.6 = (bf16[128,4096]{1,0:T(8,128)(2,1)S(1)}, bf16[128,4096]{1,0:T(8,128)(2,1)}, u32[]{:S(2)}) copy-start(bf16[128,4096]{1,0:T(8,128)(2,1)} %param.13) | copy-start | bytes 3145732
  14.8 186.8 %all-gather.9.cloned.1.call-start = ((), (), s32[]{:S(2)}) async-start(), calls=%async_computation.5 | async-start | bytes 2162688 | tf_op jit(solution)/shard_map/all_gather | solution.py:15
  27.6 1.0 copy-start.7
  33.0 89.8 %all-to-all-start = ((bf16[128,4,1024]{2,0,1:T(8,128)(2,1)}), bf16[128,4,1024]{2,0,1:T(8,128)(2,1)}, u32[]{:S(2)}, u32[]{:S(2)}) async-start(bf16[128,4,1024]{2,0,1:T(8,128)(2,1)} %bitcast.54), calls=%async_computation | async-start | bytes 2097152 | tf_op jit(solution)/shard_map/all_to_all | solution.py:111
  40.4 302.3 %all-gather.7.cloned.1.call-start = ((), (), s32[]{:S(2)}) async-start(), calls=%async_computation.4 | async-start | bytes 2162688 | tf_op jit(solution)/shard_map/all_gather | solution.py:15
  192.1 3.4 copy-start.2
  195.4 2.1 copy-start.1
  239.3 114.7 %all-to-all-start.3 = ((f32[4,128,1024]{1,2,0:T(8,128)}), f32[4,128,1024]{1,2,0:T(8,128)S(1)}, u32[]{:S(2)}, u32[]{:S(2)}) async-start(f32[4,128,1024]{1,2,0:T(8,128)} %copy.81), calls=%async_computation.3 | async-start | bytes 4194304 | tf_op jit(solution)/shard_map/all_to_all | solution.py:131
  354.1 147.7 %all-to-all-start.2 = ((f32[4,128,1024]{1,2,0:T(8,128)}), f32[4,128,1024]{1,2,0:T(8,128)}, u32[]{:S(2)}, u32[]{:S(2)}) async-start(f32[4,128,1024]{1,2,0:T(8,128)} %copy.75), calls=%async_computation.2 | async-start | bytes 4194304 | tf_op jit(solution)/shard_map/all_to_all | solution.py:130
  501.8 3.0 copy-start.3
  501.8 3.0 copy-start.5
Sparse Core Ops, SparseCore 0:
  31.8 155.5 all-gather.8
  189.1 153.5 all-gather.6
